TPU v7x, 32 devices: a whole 2x2x4 slice. The times are simulated.
32 devices in a mesh: orb: 8 (over z, y), pair: 4 (over x, core).
Axes of the slice: x: 2, y: 2, z: 4, core: 2. Of those that a mesh axis runs over, the one named last changes fastest.
Arguments:
- orbitals: float32 [16, 32, 1024], P('orb'), may hold values from -6 to 6
- send_index: int32 [8, 4, 8], P('orb', 'pair'), may hold values from -1 to 1, as said below
- pair_left: int32 [8, 4, 8], P('orb', 'pair'), may hold values from -1 to 1, as said below
- pair_offset: int32 [8, 4, 8], P('orb', 'pair'), may hold values from -8 to 8
Outputs:
- exchange_field: float32 [16, 32, 1024], P('orb', 'pair')
Inputs may be any that keep to these rules, and one draw needn't show every extreme that they name: `send_index`: -1 marks an empty route. Toward some orb index, drawn from the seed, every route from every device is live. pair_left[d, p, s + c] is -1 exactly when send_index[s, p, d + c] is -1.
All inputs are finite; a program needn't handle non-finite values.
Results may differ from a plain program's by a relative error of at most 0.0075.
Values may be sent and summed in bfloat16 or wider, within the bound.
A program may use at most 128 MiB of HBM per device.

v0:
```python
import jax
import jax.numpy as jnp
from jax import lax
from jax.sharding import PartitionSpec as P

SWEEPS = 2


pair_block = 16


def neighbours(field):
    box_side = field.shape[1]
    plane = field.shape[2]
    edge_x = jnp.zeros_like(field[:, :1])
    summed = jnp.concatenate([field[:, 1:], edge_x], 1) + jnp.concatenate(
        [edge_x, field[:, :-1]], 1
    )
    edge_y = jnp.zeros_like(field[:, :, :box_side])
    summed = (
        summed
        + jnp.concatenate([field[:, :, box_side:], edge_y], 2)
        + jnp.concatenate([edge_y, field[:, :, :-box_side]], 2)
    )
    edge_z = jnp.zeros_like(field[:, :, :1])
    column = lax.broadcasted_iota(jnp.int32, (1, 1, plane), 2) % box_side
    upper = jnp.where(column < box_side - 1, jnp.concatenate([field[:, :, 1:], edge_z], 2), 0.0)
    lower = jnp.where(column > 0, jnp.concatenate([edge_z, field[:, :, :-1]], 2), 0.0)
    return summed + upper + lower


def pair_work(left, right, offsets):
    box_side = left.shape[1]
    positions = jnp.arange(box_side, dtype=jnp.int32)
    forward = (
        positions[None, None, :] == positions[None, :, None] - offsets[:, None, None]
    ).astype(jnp.bfloat16)
    shifted_right = jnp.einsum("rxw,rwc->rxc", forward, right, preferred_element_type=jnp.float32)
    left_wide = left.astype(jnp.float32)
    density = left_wide * shifted_right
    potential = jnp.zeros_like(density)
    for sweep_number in range(SWEEPS):
        potential = (neighbours(potential) + density) / 6.0
    to_left = (potential * shifted_right).astype(jnp.bfloat16)
    backward = (
        positions[None, None, :] == positions[None, :, None] + offsets[:, None, None]
    ).astype(jnp.float32)
    to_right = jnp.einsum(
        "rxw,rwc->rxc",
        backward,
        potential * left_wide,
        precision=lax.Precision.HIGHEST,
        preferred_element_type=jnp.float32,
    )
    return (to_left, to_right.astype(jnp.bfloat16))


def run_pairs(fetch, live_mask, offsets, shape):
    slot_count = live_mask.shape[0]
    keys = jnp.where(live_mask, 0, slot_count) + jnp.arange(slot_count, dtype=jnp.int32)
    arrangement = jnp.argsort(keys)
    width = min(pair_block, slot_count)
    blocks = (jnp.sum(live_mask.astype(jnp.int32)) + width - 1) // width
    empty = jnp.zeros(shape, jnp.bfloat16)

    def advance(block_number, carried):
        start = block_number * width
        chosen = lax.dynamic_slice_in_dim(arrangement, start, width, 0)
        part_left, part_right = fetch(chosen)
        out_left, out_right = pair_work(part_left, part_right, jnp.take(offsets, chosen, 0))
        return (carried[0].at[chosen].set(out_left), carried[1].at[chosen].set(out_right))

    return lax.fori_loop(0, blocks, advance, (empty, empty))


def collect(values, targets, owned):
    selector = (targets[None, :] == jnp.arange(owned, dtype=jnp.int32)[:, None]).astype(
        jnp.bfloat16
    )
    flat = values.reshape(values.shape[0], -1)
    return jnp.dot(selector, flat, preferred_element_type=jnp.float32)


def local(orbitals, send_index, pair_left, pair_offset):
    owned = orbitals.shape[0]
    box_side = orbitals.shape[1]
    plane = orbitals.shape[2]
    send_rows = send_index.reshape(-1)
    left_rows = pair_left.reshape(-1)
    offsets = pair_offset.reshape(-1)
    slot_count = send_rows.shape[0]
    n_orb = lax.axis_size("orb")
    per_peer = slot_count // n_orb
    shape = (slot_count, box_side, plane)
    rounded = orbitals.astype(jnp.bfloat16)
    padded_boxes = jnp.concatenate([rounded, jnp.zeros((1, box_side, plane), jnp.bfloat16)], 0)
    send_pick = jnp.where(send_rows >= 0, send_rows, owned)
    left_pick = jnp.where(left_rows >= 0, left_rows, owned)
    left_live = left_rows >= 0

    def local_boxes(picks, chosen):
        return jnp.take(padded_boxes, jnp.take(picks, chosen, 0), 0)

    outgoing = jnp.take(padded_boxes, send_pick, 0)
    arrived = lax.all_to_all(
        outgoing.reshape(n_orb, per_peer, box_side, plane),
        "orb",
        split_axis=0,
        concat_axis=0,
        tiled=True,
    )
    arrived = arrived.reshape(shape)

    def fetch_owner(chosen):
        return (local_boxes(left_pick, chosen), jnp.take(arrived, chosen, 0))

    to_left, to_right = run_pairs(fetch_owner, left_live, offsets, shape)
    returned = lax.all_to_all(
        to_right.reshape(n_orb, per_peer, box_side, plane),
        "orb",
        split_axis=0,
        concat_axis=0,
        tiled=True,
    )
    returned = returned.reshape(shape)
    accumulated = collect(to_left, left_rows, owned) + collect(returned, send_rows, owned)
    accumulated = accumulated.reshape(owned, box_side, plane)
    field = lax.psum_scatter(
        accumulated.astype(jnp.bfloat16), "pair", scatter_dimension=1, tiled=True
    ).astype(jnp.float32)
    return -0.25 * field


def solution(mesh):
    return jax.shard_map(
        local,
        mesh=mesh,
        in_specs=(
            P("orb", None, None),
            P("orb", "pair", None),
            P("orb", "pair", None),
            P("orb", "pair", None),
        ),
        out_specs=P("orb", "pair", None),
        check_vma=False,
    )
```

profile of v0, /device:TPU:0, one launch (start us, length us, event | category | flops | bytes accessed | tf_op | source)
XLA Modules:
  0.0 90.1 jit_solution(1625989211330670326)
XLA Ops:
  6.5 0.7 compare_and_fusion.4
  7.3 1.0 %convert_element_type.50 = bf16[2,32,1024]{2,1,0:T(8,128)(2,1)S(1)} convert(f32[2,32,1024]{2,1,0:T(8,128)} %param.8) | non-fusion elementwise | flops 65536 | bytes 393216 | tf_op jit(solution)/shard_map/convert_element_type | solution.py:95
  8.3 0.6 gather_fusion.2
  8.9 0.9 %bitcast_select_fusion = bf16[8,1,32,1024]{3,2,1,0:T(8,128)(2,1)} fusion(bf16[8,32,1024]{2,1,0:T(8,128)(2,1)S(1)} %gather_fusion.2, pred[8]{0:T(512)(128)(4,1)S(1)} %compare_and_fusion.4), kind=kLoop, calls=%fused_computation.59 | loop fusion | flops 262144 | bytes 1048584 | tf_op jit(solution)/shard_map/jit(_take)/select_n | solution.py:104
  9.8 7.4 %all-to-all-start = ((bf16[8,1,32,1024]{3,2,1,0:T(8,128)(2,1)}), bf16[8,1,32,1024]{3,2,1,0:T(8,128)(2,1)S(1)}, u32[]{:S(2)}, u32[]{:S(2)}) async-start(bf16[8,1,32,1024]{3,2,1,0:T(8,128)(2,1)} %bitcast_select_fusion), calls=%async_computation | async-start | bytes 1048576 | tf_op jit(solution)/shard_map/all_to_all | solution.py:105
  17.2 0.6 compare_select_fusion.10
  17.9 1.0 %sort.17 = (s32[8]{0:T(128)}, s32[8]{0:T(128)S(1)}) sort(s32[8]{0:T(128)S(1)} %get-tuple-element.290, s32[8]{0:T(128)S(1)} %iota.76), dimensions={0}, to_apply=%region_1.2 | sort | flops 24 | bytes 128 | tf_op jit(solution)/shard_map/jit(argsort)/sort | solution.py:61
  18.9 0.6 gather_fusion.5
  20.3 0.6 gather_fusion.6
  21.0 0.6 gather_fusion.3
  21.7 10.0 %all-to-all-done = bf16[8,1,32,1024]{3,2,1,0:T(8,128)(2,1)S(1)} async-done(((bf16[8,1,32,1024]{3,2,1,0:T(8,128)(2,1)}), bf16[8,1,32,1024]{3,2,1,0:T(8,128)(2,1)S(1)}, u32[]{:S(2)}, u32[]{:S(2)}) %all-to-all-start) | async-done | bytes 524320 | tf_op jit(solution)/shard_map/all_to_all | solution.py:105
  31.7 0.6 gather_fusion.4
  32.3 0.4 add_multiply_fusion.1
  32.7 0.4 fusion.61
  33.1 0.4 fusion.62
  33.7 1.4 %convolution_convert_fusion = bf16[8,32,1024]{2,1,0:T(8,128)(2,1)S(1)} fusion(f32[8,32,1024]{2,1,0:T(8,128)S(1)} %get-tuple-element.292, f32[8,32,1023]{2,1,0:T(8,128)S(1)} %get-tuple-element.285, f32[8,32,1023]{2,1,0:T(8,128)S(1)} %get-tuple-element.284, f32[8,32,992]{2,1,0:T(8,128)S(1)} %get-tuple-element.283, f32[8,32,992]{2,1,0:T(8,128)S(1)} %get-tuple-element.282, ...), kind=kOutput, calls=%fused_computation.42 | convolution fusion | flops 104079360 | bytes 8258568 | tf_op jit(solution)/shard_map/while/body/rxw,rwc->rxc/dot_general | solution.py:48
  35.1 0.9 broadcast_in_dim.145.clone
  36.1 7.3 %while.17 = (s32[]{:T(128)}, bf16[8,32,1024]{2,1,0:T(8,128)(2,1)S(1)}, bf16[8,32,1024]{2,1,0:T(8,128)(2,1)}, s32[]{:T(128)}, s32[8]{0:T(128)S(1)}, /*index=5*/s3...) while((s32[]{:T(128)}, ...), condition=%wide.region_5.7_spmd, body=%wide.region_2.6_spmd.sunk | while | flops 23087504 | bytes 29018188 | solution.py:73
  36.3 0.6 gather_fusion
  36.9 0.6 gather_fusion.1
  37.5 2.5 %scatter_fusion.1 = bf16[8,32,1024]{2,1,0:T(8,128)(2,1)} fusion(bf16[8,32,1024]{2,1,0:T(8,128)(2,1)} %get-tuple-element.399, s32[8]{0:T(128)S(1)} %get-tuple-element.371, bf16[8,32,1024]{2,1,0:T(8,128)(2,1)S(1)} %get-tuple-element.418), kind=kCustom, calls=%fused_computation.8.clone.1 | custom fusion | bytes 1572896 | tf_op jit(solution)/shard_map/while/body/scatter | solution.py:71
  39.9 0.4 add_multiply_fusion.3
  40.5 0.4 fusion.73
  40.9 0.4 fusion.72
  41.3 1.3 %multiply_convert_fusion.2 = bf16[8,32,1024]{2,1,0:T(8,128)(2,1)S(1)} fusion(f32[8,32,1024]{2,1,0:T(8,128)S(1)} %get-tuple-element.376, f32[8,32,1023]{2,1,0:T(8,128)S(1)} %get-tuple-element.378, f32[8,32,1023]{2,1,0:T(8,128)S(1)} %get-tuple-element.379, f32[8,32,992]{2,1,0:T(8,128)S(1)} %get-tuple-element.380, ...), kind=kLoop, calls=%fused_computation.9.clone.1 | loop fusion | flops 3670016 | bytes 8257544 | tf_op jit(solution)/shard_map/while/body/convert_element_type | solution.py:44
  42.6 0.8 scatter_fusion
  43.4 3.7 %all-to-all-start.1 = ((bf16[8,1,32,1024]{3,2,1,0:T(8,128)(2,1)}), bf16[8,1,32,1024]{3,2,1,0:T(8,128)(2,1)S(1)}, u32[]{:S(2)}, u32[]{:S(2)}) async-start(bf16[8,1,32,1024]{3,2,1,0:T(8,128)(2,1)} %bitcast.11), calls=%async_computation.1 | async-start | bytes 1048576 | tf_op jit(solution)/shard_map/all_to_all | solution.py:118
  47.7 14.0 %all-to-all-done.1 = bf16[8,1,32,1024]{3,2,1,0:T(8,128)(2,1)S(1)} async-done(((bf16[8,1,32,1024]{3,2,1,0:T(8,128)(2,1)}), bf16[8,1,32,1024]{3,2,1,0:T(8,128)(2,1)S(1)}, u32[]{:S(2)}, u32[]{:S(2)}) %all-to-all-start.1) | async-done | bytes 524320 | tf_op jit(solution)/shard_map/all_to_all | solution.py:118
  62.3 0.7 copy.9
  63.0 18.9 %reduce-scatter.4.cloned.1.call-done = bf16[8,2048]{1,0:T(8,128)(2,1)} async-done(((bf16[32,2048]{1,0:T(8,128)(2,1)}), bf16[8,2048]{1,0:T(8,128)(2,1)}) %reduce-scatter.4.cloned.1.call-update) | async-done | bytes 32784
  81.8 0.8 reshape.281
  82.6 0.6 convert_multiply_fusion.3
  (49 shorter events, 2.0 us)
Async XLA Ops:
  6.5 13.7 %copy-start = (s32[1,1,8]{2,1,0:T(1,128)S(1)}, s32[1,1,8]{2,1,0:T(1,128)}, u32[]{:S(2)}) copy-start(s32[1,1,8]{2,1,0:T(1,128)} %param.11) | copy-start | bytes 100
  6.5 0.7 copy-start.2
  9.8 7.4 %copy-start.1 = (s32[1,1,8]{2,1,0:T(1,128)S(1)}, s32[1,1,8]{2,1,0:T(1,128)}, u32[]{:S(2)}) copy-start(s32[1,1,8]{2,1,0:T(1,128)} %param.10) | copy-start | bytes 100
  9.8 21.9 %all-to-all-start = ((bf16[8,1,32,1024]{3,2,1,0:T(8,128)(2,1)}), bf16[8,1,32,1024]{3,2,1,0:T(8,128)(2,1)S(1)}, u32[]{:S(2)}, u32[]{:S(2)}) async-start(bf16[8,1,32,1024]{3,2,1,0:T(8,128)(2,1)} %bitcast_select_fusion), calls=%async_computation | async-start | bytes 1048576 | tf_op jit(solution)/shard_map/all_to_all | solution.py:105
  43.4 18.3 %all-to-all-start.1 = ((bf16[8,1,32,1024]{3,2,1,0:T(8,128)(2,1)}), bf16[8,1,32,1024]{3,2,1,0:T(8,128)(2,1)S(1)}, u32[]{:S(2)}, u32[]{:S(2)}) async-start(bf16[8,1,32,1024]{3,2,1,0:T(8,128)(2,1)} %bitcast.11), calls=%async_computation.1 | async-start | bytes 1048576 | tf_op jit(solution)/shard_map/all_to_all | solution.py:118
  47.0 34.8 %reduce-scatter.4.cloned.1.call-start = ((), (), s32[]{:S(2)}) async-start(), calls=%async_computation.3 | async-start | bytes 163840
Sparse Core Ops, SparseCore 0:
  63.1 18.6 reduce-scatter.3
where the time goes:
time: 90.6 us; the launch traced here: 90.1 us
  waiting for transfers between devices  42.9 us (47%)
  between operations  14.3 us (16%)
  local copies, waits for them, and re-layouts  12.4 us (14%)
  starting transfers between devices  11.1 us (12%)
  other arithmetic  6.42 us (7%)
  matrix products  2.8 us (3%)
    unnamed x2, waiting for transfers between devices  18.9 us
    all_to_all x1, waiting for transfers between devices, local(): lax.all_to_all(to_right.reshape(n_orb, per_peer, box_side, plane), 'orb',...  14 us
    all_to_all x1, waiting for transfers between devices, local(): lax.all_to_all(outgoing.reshape(n_orb, per_peer, box_side, plane), 'orb',...  10 us
    all_to_all x1, starting transfers between devices, local(): lax.all_to_all(outgoing.reshape(n_orb, per_peer, box_side, plane), 'orb',...  7.44 us
    all_to_all x1, starting transfers between devices, local(): lax.all_to_all(to_right.reshape(n_orb, per_peer, box_side, plane), 'orb',...  3.65 us
    scatter x1, local copies, waits for them, and re-layouts, advance(): carried[1].at[chosen].set(out_right)  2.47 us
    unnamed x10, local copies, waits for them, and re-layouts  2.05 us
  transfers between devices with their start and end apart: 3, of which 3 were waited for; matrix products, arithmetic and copies ran while one was open for 5% of the time, Pallas kernels for 0%

commit v1 on v0

v1 whole, which is shorter than its diff:
```python
import functools

import jax
import jax.numpy as jnp
from jax import lax
from jax.experimental import pallas as pl
from jax.experimental.pallas import tpu as pltpu
from jax.sharding import PartitionSpec as P

LANES = 128
TAG = 16


def in_plane(q, box_side, lane, sub):
    group = q.shape[0]
    up = jnp.where(lane % box_side > 0, pltpu.roll(q, 1, 1), 0.0)
    down = jnp.where(lane % box_side < box_side - 1, pltpu.roll(q, LANES - 1, 1), 0.0)
    ahead = pltpu.roll(q, box_side, 1)
    ahead = jnp.where(
        lane >= box_side, ahead, jnp.where(sub > 0, pltpu.roll(ahead, 1, 0), 0.0)
    )
    behind = pltpu.roll(q, LANES - box_side, 1)
    behind = jnp.where(
        lane < LANES - box_side,
        behind,
        jnp.where(sub < group - 1, pltpu.roll(behind, group - 1, 0), 0.0),
    )
    return (up + down) + (ahead + behind)


def kernel(
    n_orb,
    n_pair,
    orb_ref,
    send_ref,
    left_ref,
    off_ref,
    out_ref,
    staged,
    boxes,
    padded_right,
    product,
    left_sum,
    out_a,
    in_a,
    out_b,
    in_b,
    out_l,
    in_l,
    out_d,
    in_d,
    own_d,
    send_a,
    recv_a,
    send_b,
    recv_b,
    send_l,
    recv_l,
    send_d,
    recv_d,
):
    owned, box_side, plane = orb_ref.shape
    group = plane // LANES
    pad = box_side // 4
    own_rows = box_side // n_pair
    part_rows = own_rows * group
    me = lax.axis_index("orb")
    my_pair = lax.axis_index("pair")

    barrier = pltpu.get_barrier_semaphore()

    def greet_orb(k, c):
        pl.semaphore_signal(barrier, inc=1, device_id={"orb": lax.rem(me + k, n_orb)})
        return c

    def greet_pair(k, c):
        pl.semaphore_signal(barrier, inc=1, device_id={"pair": lax.rem(my_pair + k, n_pair)})
        return c

    lax.fori_loop(1, n_orb, greet_orb, 0)
    lax.fori_loop(1, n_pair, greet_pair, 0)

    for b in range(owned):
        for c in range(group):
            piece = orb_ref[b, :, c * LANES : (c + 1) * LANES]
            staged[pl.ds(b * box_side * group + c, box_side, stride=group), :] = piece
    boxes[:box_side] = jnp.zeros((box_side, group, LANES), jnp.float32)
    for i in range(owned * box_side // 8):
        piece = staged[pl.ds(i * 8 * group, 8 * group), :]
        piece = piece.astype(jnp.bfloat16).astype(jnp.float32)
        boxes[pl.ds(box_side + i * 8, 8)] = piece.reshape(8, group, LANES)
    zeros = jnp.zeros((pad, group, LANES), jnp.float32)
    for ref in (padded_right, product):
        ref[:pad] = zeros
        ref[pad + box_side :] = zeros
    left_sum[...] = jnp.zeros(left_sum.shape, jnp.float32)

    def select(peer, dst):
        pick = send_ref[0, 0, peer]
        base = (pick + 1) * box_side
        for i in range(box_side // 8):
            v = boxes[pl.ds(base + i * 8, 8)].reshape(8 * group, LANES)
            dst[pl.ds(i * 8 * group, 8 * group), :] = v.astype(jnp.bfloat16)
        dst[pl.ds(box_side * group, TAG), :] = jnp.full(
            (TAG, LANES), pick, jnp.int32
        ).astype(jnp.float32).astype(jnp.bfloat16)

    def build(k, c):
        peer = lax.rem(me + k, n_orb)
        select(peer, out_a.at[peer])
        return c

    lax.fori_loop(1, n_orb, build, 0)
    select(me, in_a.at[me])
    pl.semaphore_wait(barrier, n_orb - 1 + n_pair - 1)

    def copy_a(src, dst, peer):
        return pltpu.make_async_remote_copy(
            src_ref=out_a.at[src],
            dst_ref=in_a.at[dst],
            send_sem=send_a.at[src],
            recv_sem=recv_a.at[dst],
            device_id={"orb": peer},
        )

    def start_a(k, c):
        peer = lax.rem(me + k, n_orb)
        copy_a(peer, me, peer).start()
        return c

    lax.fori_loop(1, n_orb, start_a, 0)

    lane = lax.broadcasted_iota(jnp.int32, (group, LANES), 1)
    sub = lax.broadcasted_iota(jnp.int32, (group, LANES), 0)
    sixth = 1.0 / 6.0

    def copy_b(s, q, dst):
        return pltpu.make_async_remote_copy(
            src_ref=out_b.at[s, q],
            dst_ref=in_b.at[s, dst],
            send_sem=send_b.at[s, q],
            recv_sem=recv_b.at[s, dst],
            device_id={"pair": q},
        )

    def compute(s):
        t = off_ref[0, 0, s]
        pick = left_ref[0, 0, s]
        base = (pick + 1) * box_side
        picked = jnp.full((group, LANES), pick, jnp.int32)
        masks = [picked == b for b in range(owned)]
        for i in range(box_side // 8):
            v = in_a[s, pl.ds(i * 8 * group, 8 * group), :].astype(jnp.float32)
            padded_right[pl.ds(pad + i * 8, 8)] = v.reshape(8, group, LANES)

        def load(x):
            right = padded_right[pad + x - t]
            left = boxes[base + x]
            return left, right, left * right

        nothing = jnp.zeros((group, LANES), jnp.float32)
        previous, (left, right, q) = nothing, load(0)
        for x in range(box_side):
            later = load(x + 1) if x + 1 < box_side else (None, None, nothing)
            around = in_plane(q, box_side, lane, sub) + (previous + later[2])
            potential = (around * sixth + q) * sixth
            to_left = potential * right
            for b in range(owned):
                row = b * box_side + x
                left_sum[row] = left_sum[row] + jnp.where(masks[b], to_left, 0.0)
            product[pad + x] = potential * left
            previous, (left, right, q) = q, later
        for q in range(n_pair):
            v = product[pl.ds(pad + q * own_rows + t, own_rows)]
            out_b[s, q, pl.ds(0, part_rows), :] = v.reshape(part_rows, LANES).astype(jnp.bfloat16)
            out_b[s, q, pl.ds(part_rows, TAG), :] = in_a[s, pl.ds(box_side * group, TAG), :]

        def send(j, c):
            copy_b(s, lax.rem(my_pair + j, n_pair), my_pair).start()
            return c

        lax.fori_loop(1, n_pair, send, 0)

    def gathered(s):
        def wait(j, c):
            copy_b(s, lax.rem(my_pair + j, n_pair), lax.rem(my_pair + j, n_pair)).wait_recv()
            return c

        lax.fori_loop(1, n_pair, wait, 0)

        total = [jnp.zeros((part_rows, LANES), jnp.float32) for _ in range(owned)]
        for j in range(n_pair):
            if j == 0:
                block = out_b[s, my_pair, :, :]
            else:
                block = in_b[s, lax.rem(my_pair + j, n_pair), :, :]
            value = block[:part_rows].astype(jnp.float32)
            tag = block[part_rows : part_rows + 8 * 2].astype(jnp.float32)[:8]
            for b in range(owned):
                mask = jnp.concatenate([tag == b] * (part_rows // 8), 0)
                total[b] = total[b] + jnp.where(mask, value, 0.0)
        return total

    def copy_d(src, dst, peer):
        return pltpu.make_async_remote_copy(
            src_ref=out_d.at[src],
            dst_ref=in_d.at[dst],
            send_sem=send_d.at[src],
            recv_sem=recv_d.at[dst],
            device_id={"orb": peer},
        )

    def finish(s):
        total = gathered(s)
        for b in range(owned):
            out_d[s, pl.ds(b * part_rows, part_rows), :] = total[b].astype(jnp.bfloat16)
        copy_d(s, me, s).start()

    compute(me)

    def step(k, c):
        s = lax.rem(me + n_orb - k, n_orb)
        copy_a(s, s, s).wait_recv()
        compute(s)

        @pl.when(k > 1)
        def _():
            finish(lax.rem(me + n_orb - k + 1, n_orb))

        return c

    lax.fori_loop(1, n_orb, step, 0)

    def copy_l(q, dst):
        return pltpu.make_async_remote_copy(
            src_ref=out_l.at[q],
            dst_ref=in_l.at[dst],
            send_sem=send_l.at[q],
            recv_sem=recv_l.at[dst],
            device_id={"pair": q},
        )

    for q in range(n_pair):
        for b in range(owned):
            v = left_sum[pl.ds(b * box_side + q * own_rows, own_rows)]
            out_l[q, pl.ds(b * part_rows, part_rows), :] = v.reshape(part_rows, LANES).astype(
                jnp.bfloat16
            )

    def send_left(j, c):
        copy_l(lax.rem(my_pair + j, n_pair), my_pair).start()
        return c

    lax.fori_loop(1, n_pair, send_left, 0)
    finish(lax.rem(me + 1, n_orb))

    total = gathered(me)

    def wait_left(j, c):
        q = lax.rem(my_pair + j, n_pair)
        copy_l(q, q).wait_recv()
        return c

    lax.fori_loop(1, n_pair, wait_left, 0)
    for b in range(owned):
        rows = pl.ds(b * part_rows, part_rows)
        value = total[b] + out_l[my_pair, rows, :].astype(jnp.float32)
        for j in range(1, n_pair):
            value = value + in_l[lax.rem(my_pair + j, n_pair), rows, :].astype(jnp.float32)
        own_d[rows, :] = value

    def add(k, c):
        s = lax.rem(me + n_orb - k, n_orb)
        copy_d(s, s, s).wait_recv()
        own_d[...] = own_d[...] + in_d[s, :, :].astype(jnp.float32)
        return c

    lax.fori_loop(1, n_orb, add, 0)
    for b in range(owned):
        for c in range(group):
            out_ref[b, :, c * LANES : (c + 1) * LANES] = own_d[
                pl.ds(b * part_rows + c, own_rows, stride=group), :
            ]

    def drain(k, c):
        peer = lax.rem(me + k, n_orb)
        copy_a(peer, me, peer).wait_send()
        copy_d(peer, me, peer).wait_send()
        return c

    lax.fori_loop(1, n_orb, drain, 0)

    def drain_pairs(s, c):
        def one(j, c):
            copy_b(s, lax.rem(my_pair + j, n_pair), my_pair).wait_send()
            return c

        return lax.fori_loop(1, n_pair, one, c)

    lax.fori_loop(0, n_orb, drain_pairs, 0)

    def drain_left(j, c):
        copy_l(lax.rem(my_pair + j, n_pair), my_pair).wait_send()
        return c

    lax.fori_loop(1, n_pair, drain_left, 0)


def local(n_orb, n_pair, orbitals, send_index, pair_left, pair_offset):
    owned, box_side, plane = orbitals.shape
    group = plane // LANES
    pad = box_side // 4
    rows = box_side * group
    part_rows = rows // n_pair
    smem = pl.BlockSpec(memory_space=pltpu.SMEM)
    vmem = pl.BlockSpec(memory_space=pltpu.VMEM)
    bf16, f32 = jnp.bfloat16, jnp.float32
    dma = pltpu.SemaphoreType.DMA
    field = pl.pallas_call(
        functools.partial(kernel, n_orb, n_pair),
        out_shape=jax.ShapeDtypeStruct((owned, box_side // n_pair, plane), f32),
        in_specs=[vmem, smem, smem, smem],
        out_specs=vmem,
        scratch_shapes=[
            pltpu.VMEM((owned * rows, LANES), f32),
            pltpu.VMEM(((owned + 1) * box_side, group, LANES), f32),
            pltpu.VMEM((box_side + 2 * pad, group, LANES), f32),
            pltpu.VMEM((box_side + 2 * pad, group, LANES), f32),
            pltpu.VMEM((owned * box_side, group, LANES), f32),
            pltpu.VMEM((n_orb, rows + TAG, LANES), bf16),
            pltpu.VMEM((n_orb, rows + TAG, LANES), bf16),
            pltpu.VMEM((n_orb, n_pair, part_rows + TAG, LANES), bf16),
            pltpu.VMEM((n_orb, n_pair, part_rows + TAG, LANES), bf16),
            pltpu.VMEM((n_pair, owned * part_rows, LANES), bf16),
            pltpu.VMEM((n_pair, owned * part_rows, LANES), bf16),
            pltpu.VMEM((n_orb, owned * part_rows, LANES), bf16),
            pltpu.VMEM((n_orb, owned * part_rows, LANES), bf16),
            pltpu.VMEM((owned * part_rows, LANES), f32),
            dma((n_orb,)),
            dma((n_orb,)),
            dma((n_orb, n_pair)),
            dma((n_orb, n_pair)),
            dma((n_pair,)),
            dma((n_pair,)),
            dma((n_orb,)),
            dma((n_orb,)),
        ],
        compiler_params=pltpu.CompilerParams(
            collective_id=0, has_side_effects=True, vmem_limit_bytes=67043328 if n_orb > 32 else None
        ),
        name="exchange",
    )(orbitals, send_index, pair_left, pair_offset)
    return -0.25 * field


def solution(mesh):
    n_orb, n_pair = mesh.shape["orb"], mesh.shape["pair"]
    return jax.shard_map(
        functools.partial(local, n_orb, n_pair),
        mesh=mesh,
        in_specs=(
            P("orb", None, None),
            P("orb", "pair", None),
            P("orb", "pair", None),
            P("orb", "pair", None),
        ),
        out_specs=P("orb", "pair", None),
        check_vma=False,
    )
```

time: 90.6 us -> 37.4 us (0.41)
  waiting for transfers between devices: 42.9 us -> 0 us
  Pallas kernels: 0 us -> 35.8 us
  between operations: 14.3 us -> 0.01 us
  local copies, waits for them, and re-layouts: 12.4 us -> 0 us
  starting transfers between devices: 11.1 us -> 0 us
  other arithmetic: 6.42 us -> 1.47 us
  matrix products: 2.8 us -> 0 us
    pallas_call x0 -> x1, Pallas kernels: none -> 35.8 us  [local(): pl.pallas_call(functools.partial(kernel, n_orb, n_pair), out_shape=jax.Sh...]
    all_to_all x2 -> x0, waiting for transfers between devices: 24.1 us -> none  [the longest x1 14 us: local(): lax.all_to_all(to_right.reshape(n_orb, per_peer, box_side, plane), 'orb',...]
    unnamed x2 -> x0, waiting for transfers between devices: 18.9 us -> none
    all_to_all x2 -> x0, starting transfers between devices: 11.1 us -> none  [the longest x1 7.44 us: local(): lax.all_to_all(outgoing.reshape(n_orb, per_peer, box_side, plane), 'orb',...]
    gather x7 -> x0, local copies, waits for them, and re-layouts: 4.18 us -> none  [the longest x3 1.8 us: local_boxes(): return jnp.take(padded_boxes, jnp.take(picks, chosen, 0), 0)]
    scatter x2 -> x0, local copies, waits for them, and re-layouts: 3.26 us -> none  [the longest x1 2.47 us: advance(): carried[1].at[chosen].set(out_right)]
    dot_general x5 -> x0, matrix products: 2.8 us -> none  [the longest x1 1.45 us: pair_work(): jnp.einsum('rxw,rwc->rxc', backward, potential * left_wide, precision=lax...]
    convert_element_type x2 -> x0, other arithmetic: 2.25 us -> none  [the longest x1 1.28 us: pair_work(): to_left = (potential * shifted_right).astype(jnp.bfloat16)]
  transfers between devices with their start and end apart: 3 -> 0, of which waited for: 3 -> 0; matrix products, arithmetic and copies ran while one was open for 5% -> 0% of each run, Pallas kernels for 0% -> 0%
where the time goes in v1:
time: 37.4 us; the launch traced here: 37.2 us
  Pallas kernels  35.8 us (96%)
  other arithmetic  1.47 us (4%)
    pallas_call x1, Pallas kernels, local(): pl.pallas_call(functools.partial(kernel, n_orb, n_pair), out_shape=jax.Sh...  35.8 us
    mul x1, other arithmetic, local(): return -0.25 * field  1.47 us

profile of v1, /device:TPU:0, one launch (start us, length us, event | category | flops | bytes accessed | tf_op | source)
XLA Modules:
  0.0 37.2 jit_solution(7471099208118830727)
XLA Ops:
  0.0 35.8 %exchange.1 = f32[2,8,1024]{2,1,0:T(8,128)} custom-call(f32[2,32,1024]{2,1,0:T(8,128)} %orb_ref.1, s32[1,1,8]{2,1,0:T(1,128)} %send_ref.1, s32[1,1,8]{2,1,0:T(1,128)} %left_ref.1, s32[1,1,8]{2,1,0:T(1,128)} %off_ref.1), custom_call_target="tpu_custom_call" | custom-call | tf_op jit(solution)/shard_map/exchange/pallas_call | solution.py:319
  35.8 1.5 %broadcast_multiply_fusion = f32[2,8,1024]{2,1,0:T(8,128)} fusion(f32[2,8,1024]{2,1,0:T(8,128)} %exchange.1), kind=kLoop, calls=%fused_computation | loop fusion | flops 16384 | bytes 131072 | tf_op jit(solution)/shard_map/mul | solution.py:353

commit v2 on v0

v2 whole, which is shorter than its diff:
```python
import functools

import jax
import jax.numpy as jnp
from jax import lax
from jax.experimental import pallas as pl
from jax.experimental.pallas import tpu as pltpu
from jax.sharding import PartitionSpec as P

LANES = 128
SUBS = 8
SEND, LEFT, OFFSET = 0, 1, 2


def kernel(
    n_orb,
    n_pair,
    orb_ref,
    send_ref,
    left_ref,
    off_ref,
    out_ref,
    left_boxes,
    right_boxes,
    dens,
    prod,
    left_sum,
    right_sum,
    in_a,
    out_d,
    in_d,
    out_t,
    in_t,
    tab_pair,
    tab_orb,
    idx_pair,
    idx_orb,
    send_a,
    recv_a,
    send_d,
    recv_d,
    send_t,
    recv_t,
    send_p,
    recv_p,
    send_i,
    recv_i,
    local_sem,
):
    owned, box_side, plane = orb_ref.shape
    groups = plane // n_pair // LANES
    pad = box_side // 4
    own_rows = box_side // n_pair
    f32, bf16 = jnp.float32, jnp.bfloat16
    me = lax.axis_index("orb")
    mine = lax.axis_index("pair")
    barrier = pltpu.get_barrier_semaphore()

    def each_orb(body):
        lax.fori_loop(1, n_orb, lambda k, c: (body(lax.rem(me + k, n_orb)), c)[1], 0)

    def each_back(body):
        lax.fori_loop(1, n_orb, lambda k, c: (body(lax.rem(me + n_orb - k, n_orb)), c)[1], 0)

    def each_pair(body):
        lax.fori_loop(1, n_pair, lambda k, c: (body(lax.rem(mine + k, n_pair)), c)[1], 0)

    each_orb(lambda o: pl.semaphore_signal(barrier, inc=1, device_id={"orb": o}))
    each_pair(lambda q: pl.semaphore_signal(barrier, inc=1, device_id={"pair": q}))

    tab_pair[SEND, mine] = send_ref[0]
    tab_pair[LEFT, mine] = left_ref[0]
    tab_pair[OFFSET, mine] = off_ref[0]

    lane = lax.broadcasted_iota(jnp.int32, (box_side, LANES), 1)
    first = mine * groups
    below = jnp.maximum(first - 1, 0)
    above = jnp.minimum(first + groups, groups * n_pair - 1)

    def column(b, c):
        at = pl.ds(pl.multiple_of(c * LANES, LANES), LANES)
        return orb_ref[b, :, at].astype(bf16).astype(f32)

    left_boxes[0] = jnp.zeros(left_boxes.shape[1:], f32)
    right_boxes[...] = jnp.zeros(right_boxes.shape, f32)
    halos = []
    for b in range(owned):
        for g in range(groups):
            piece = column(b, first + g)
            left_boxes[b + 1, g] = piece
            in_a[me, b * groups + g] = piece.astype(bf16)
        has_below = lane + jnp.where(mine > 0, 0, LANES) < box_side
        has_above = lane - jnp.where(mine < n_pair - 1, 0, LANES) >= LANES - box_side
        halo = jnp.where(has_below, pltpu.roll(column(b, below), box_side, 1), 0.0)
        halo = jnp.where(
            has_above, pltpu.roll(column(b, above), LANES - box_side, 1), halo
        )
        left_boxes[b + 1, groups] = halo
        halos.append(halo if b == 0 else pltpu.roll(halo, b * 2 * box_side, 1))
    in_a[me, owned * groups] = functools.reduce(jnp.add, halos).astype(bf16)
    dens[...] = jnp.zeros(dens.shape, f32)
    prod[...] = jnp.zeros(prod.shape, f32)
    left_sum[...] = jnp.zeros(left_sum.shape, f32)

    pl.semaphore_wait(barrier, n_orb - 1 + n_pair - 1)

    def copy_p(q, row):
        return pltpu.make_async_remote_copy(
            src_ref=tab_pair.at[:, mine],
            dst_ref=tab_pair.at[:, row],
            send_sem=send_p.at[q],
            recv_sem=recv_p.at[row],
            device_id={"pair": q},
        )

    def copy_a(o, slot):
        return pltpu.make_async_remote_copy(
            src_ref=in_a.at[me],
            dst_ref=in_a.at[slot],
            send_sem=send_a.at[o],
            recv_sem=recv_a.at[slot],
            device_id={"orb": o},
        )

    def copy_i(o, slot):
        return pltpu.make_async_remote_copy(
            src_ref=tab_pair.at[SEND],
            dst_ref=tab_orb.at[slot],
            send_sem=send_i.at[o],
            recv_sem=recv_i.at[slot],
            device_id={"orb": o},
        )

    def copy_d(o, slot):
        return pltpu.make_async_remote_copy(
            src_ref=out_d.at[o],
            dst_ref=in_d.at[slot],
            send_sem=send_d.at[o],
            recv_sem=recv_d.at[slot],
            device_id={"orb": o},
        )

    def copy_t(q, slot):
        return pltpu.make_async_remote_copy(
            src_ref=out_t.at[q],
            dst_ref=in_t.at[slot],
            send_sem=send_t.at[q],
            recv_sem=recv_t.at[slot],
            device_id={"pair": q},
        )

    each_pair(lambda q: copy_p(q, mine).start())
    each_orb(lambda o: copy_a(o, me).start())
    each_pair(lambda q: copy_p(q, q).wait_recv())
    each_orb(lambda o: copy_i(o, me).start())
    tab_orb[me] = tab_pair[SEND]
    fetch = pltpu.make_async_copy(tab_pair, idx_pair, local_sem)
    fetch.start()
    fetch.wait()

    tile = (SUBS, LANES)
    lane = lax.broadcasted_iota(jnp.int32, tile, 1)
    inner_up = lane % box_side > 0
    inner_down = lane % box_side < box_side - 1
    from_here_up = lane >= box_side
    from_here_down = lane < LANES - box_side
    sixth = 1.0 / 6.0
    steps = box_side // SUBS

    def process(s, right_index):
        for b in range(owned):
            for g in range(groups):
                right_boxes[b + 1, g, pl.ds(pad, box_side), :] = in_a[s, b * groups + g].astype(f32)
            halo = in_a[s, owned * groups].astype(f32)
            if b:
                halo = pltpu.roll(halo, LANES - b * 2 * box_side, 1)
            right_boxes[b + 1, groups, pl.ds(pad, box_side), :] = halo
        right_sum[...] = jnp.zeros(right_sum.shape, f32)

        def route(p, c):
            right_pick = right_index(p)
            left_pick = idx_pair[LEFT, p, 0, s]
            t = idx_pair[OFFSET, p, 0, s]
            left_tile = jnp.full(tile, left_pick, jnp.int32)
            right_tile = jnp.full(tile, right_pick, jnp.int32)
            rights, lefts, q = {}, {}, {}
            for i in range(steps):
                for g in range(groups + 1):
                    right = right_boxes[right_pick + 1, g, pl.ds(pad + i * SUBS - t, SUBS), :]
                    left = left_boxes[left_pick + 1, g, pl.ds(i * SUBS, SUBS), :]
                    q[i, g] = left * right
                    if g < groups:
                        dens[g, pl.ds((i + 1) * SUBS, SUBS), :] = q[i, g]
                        rights[i, g], lefts[i, g] = right, left
            for i in range(steps):
                ups = [pltpu.roll(q[i, g], box_side, 1) for g in range(groups)]
                downs = [pltpu.roll(q[i, g], LANES - box_side, 1) for g in range(groups)]
                for g in range(groups):
                    here = q[i, g]
                    up = jnp.where(from_here_up, ups[g], ups[g - 1] if g else q[i, groups])
                    down = jnp.where(
                        from_here_down,
                        downs[g],
                        downs[g + 1] if g + 1 < groups else q[i, groups],
                    )
                    fore = jnp.where(inner_up, pltpu.roll(here, 1, 1), 0.0)
                    back = jnp.where(inner_down, pltpu.roll(here, LANES - 1, 1), 0.0)
                    before = dens[g, pl.ds((i + 1) * SUBS - 1, SUBS), :]
                    after = dens[g, pl.ds((i + 1) * SUBS + 1, SUBS), :]
                    around = (up + down) + (fore + back) + (before + after)
                    potential = (around * sixth + here) * sixth
                    to_left = potential * rights[i, g]
                    at = pl.ds(i * SUBS, SUBS)
                    for b in range(owned):
                        left_sum[b, g, at, :] = left_sum[b, g, at, :] + jnp.where(
                            left_tile == b, to_left, 0.0
                        )
                    prod[g, pl.ds(pad + i * SUBS, SUBS), :] = potential * lefts[i, g]
            for i in range(steps):
                at = pl.ds(i * SUBS, SUBS)
                for g in range(groups):
                    value = prod[g, pl.ds(pad + i * SUBS + t, SUBS), :]
                    for b in range(owned):
                        right_sum[b, g, at, :] = right_sum[b, g, at, :] + jnp.where(
                            right_tile == b, value, 0.0
                        )
            return c

        lax.fori_loop(0, n_pair, route, 0)

    process(me, lambda p: idx_pair[SEND, p, 0, me])
    left_sum[...] = left_sum[...] + right_sum[...]

    each_orb(lambda o: copy_i(o, o).wait_recv())
    fetch_orb = pltpu.make_async_copy(tab_orb, idx_orb, local_sem)
    fetch_orb.start()
    fetch_orb.wait()

    def slot(s):
        copy_a(s, s).wait_recv()
        process(s, lambda p: idx_orb[s, p, 0, me])
        out_d[s] = right_sum[...].astype(bf16)
        copy_d(s, me).start()

    each_back(slot)

    def add(s):
        copy_d(s, s).wait_recv()
        left_sum[...] = left_sum[...] + in_d[s].astype(f32)

    each_orb(add)

    blocks = owned * groups
    for q in range(n_pair):
        rows = left_sum[:, :, q * own_rows : (q + 1) * own_rows, :]
        out_t[q] = rows.reshape(blocks * own_rows, LANES).astype(bf16)
    in_t[mine] = out_t[mine]
    each_pair(lambda q: copy_t(q, mine).start())
    each_pair(lambda q: copy_t(q, q).wait_recv())
    for q in range(n_pair):
        rows = in_t[q].astype(f32)
        for b in range(owned):
            for g in range(groups):
                at = (b * groups + g) * own_rows
                out_ref[b, :, (q * groups + g) * LANES : (q * groups + g + 1) * LANES] = rows[
                    at : at + own_rows
                ]

    def drain_orb(o):
        copy_a(o, me).wait_send()
        copy_i(o, me).wait_send()
        copy_d(o, me).wait_send()

    def drain_pair(q):
        copy_p(q, mine).wait_send()
        copy_t(q, mine).wait_send()

    each_orb(drain_orb)
    each_pair(drain_pair)


def local(n_orb, n_pair, orbitals, send_index, pair_left, pair_offset):
    owned, box_side, plane = orbitals.shape
    slots = send_index.shape[2]
    groups = plane // n_pair // LANES
    pad = box_side // 4
    own_rows = box_side // n_pair
    assert owned * 2 * box_side == LANES and slots == n_orb
    vmem = pl.BlockSpec(memory_space=pltpu.VMEM)
    bf16, f32, i32 = jnp.bfloat16, jnp.float32, jnp.int32
    dma = pltpu.SemaphoreType.DMA
    dense = (owned, groups, box_side, LANES)
    field = pl.pallas_call(
        functools.partial(kernel, n_orb, n_pair),
        out_shape=jax.ShapeDtypeStruct((owned, own_rows, plane), f32),
        in_specs=[vmem] * 4,
        out_specs=vmem,
        scratch_shapes=[
            pltpu.VMEM((owned + 1, groups + 1, box_side, LANES), f32),
            pltpu.VMEM((owned + 1, groups + 1, box_side + 2 * pad, LANES), f32),
            pltpu.VMEM((groups, box_side + 2 * SUBS, LANES), f32),
            pltpu.VMEM((groups, box_side + 2 * pad, LANES), f32),
            pltpu.VMEM(dense, f32),
            pltpu.VMEM(dense, f32),
            pltpu.VMEM((n_orb, owned * groups + 1, box_side, LANES), bf16),
            pltpu.VMEM((n_orb, *dense), bf16),
            pltpu.VMEM((n_orb, *dense), bf16),
            pltpu.VMEM((n_pair, owned * groups * own_rows, LANES), bf16),
            pltpu.VMEM((n_pair, owned * groups * own_rows, LANES), bf16),
            pltpu.VMEM((3, n_pair, 1, slots), i32),
            pltpu.VMEM((n_orb, n_pair, 1, slots), i32),
            pltpu.SMEM((3, n_pair, 1, slots), i32),
            pltpu.SMEM((n_orb, n_pair, 1, slots), i32),
            dma((n_orb,)),
            dma((n_orb,)),
            dma((n_orb,)),
            dma((n_orb,)),
            dma((n_pair,)),
            dma((n_pair,)),
            dma((n_pair,)),
            dma((n_pair,)),
            dma((n_orb,)),
            dma((n_orb,)),
            dma(()),
        ],
        compiler_params=pltpu.CompilerParams(collective_id=0, has_side_effects=True),
        name="exchange",
    )(orbitals, send_index, pair_left, pair_offset)
    return -0.25 * field


def solution(mesh):
    n_orb, n_pair = mesh.shape["orb"], mesh.shape["pair"]
    return jax.shard_map(
        functools.partial(local, n_orb, n_pair),
        mesh=mesh,
        in_specs=(
            P("orb", None, None),
            P("orb", "pair", None),
            P("orb", "pair", None),
            P("orb", "pair", None),
        ),
        out_specs=P("orb", "pair", None),
        check_vma=False,
    )
```

time: 90.6 us -> 31.5 us (0.35)
  waiting for transfers between devices: 42.9 us -> 0 us
  Pallas kernels: 0 us -> 29.9 us
  between operations: 14.3 us -> 0.01 us
  local copies, waits for them, and re-layouts: 12.4 us -> 0 us
  starting transfers between devices: 11.1 us -> 0 us
  other arithmetic: 6.42 us -> 1.47 us
  matrix products: 2.8 us -> 0 us
    pallas_call x0 -> x1, Pallas kernels: none -> 29.9 us  [local(): pl.pallas_call(functools.partial(kernel, n_orb, n_pair), out_shape=jax.Sh...]
    all_to_all x2 -> x0, waiting for transfers between devices: 24.1 us -> none  [the longest x1 14 us: local(): lax.all_to_all(to_right.reshape(n_orb, per_peer, box_side, plane), 'orb',...]
    unnamed x2 -> x0, waiting for transfers between devices: 18.9 us -> none
    all_to_all x2 -> x0, starting transfers between devices: 11.1 us -> none  [the longest x1 7.44 us: local(): lax.all_to_all(outgoing.reshape(n_orb, per_peer, box_side, plane), 'orb',...]
    gather x7 -> x0, local copies, waits for them, and re-layouts: 4.18 us -> none  [the longest x3 1.8 us: local_boxes(): return jnp.take(padded_boxes, jnp.take(picks, chosen, 0), 0)]
    scatter x2 -> x0, local copies, waits for them, and re-layouts: 3.26 us -> none  [the longest x1 2.47 us: advance(): carried[1].at[chosen].set(out_right)]
    dot_general x5 -> x0, matrix products: 2.8 us -> none  [the longest x1 1.45 us: pair_work(): jnp.einsum('rxw,rwc->rxc', backward, potential * left_wide, precision=lax...]
    convert_element_type x2 -> x0, other arithmetic: 2.25 us -> none  [the longest x1 1.28 us: pair_work(): to_left = (potential * shifted_right).astype(jnp.bfloat16)]
  transfers between devices with their start and end apart: 3 -> 0, of which waited for: 3 -> 0; matrix products, arithmetic and copies ran while one was open for 5% -> 0% of each run, Pallas kernels for 0% -> 0%
where the time goes in v2:
time: 31.5 us; the launch traced here: 31.3 us
  Pallas kernels  29.9 us (95%)
  other arithmetic  1.47 us (5%)
    pallas_call x1, Pallas kernels, local(): pl.pallas_call(functools.partial(kernel, n_orb, n_pair), out_shape=jax.Sh...  29.9 us
    mul x1, other arithmetic, local(): return -0.25 * field  1.47 us

profile of v2, /device:TPU:0, one launch (start us, length us, event | category | flops | bytes accessed | tf_op | source)
XLA Modules:
  0.0 31.3 jit_solution(1597958706062246951)
XLA Ops:
  0.0 29.9 %exchange.1 = f32[2,8,1024]{2,1,0:T(8,128)} custom-call(f32[2,32,1024]{2,1,0:T(8,128)} %orb_ref.1, s32[1,1,8]{2,1,0:T(1,128)} %send_ref.1, s32[1,1,8]{2,1,0:T(1,128)} %left_ref.1, s32[1,1,8]{2,1,0:T(1,128)} %off_ref.1), custom_call_target="tpu_custom_call" | custom-call | tf_op jit(solution)/shard_map/exchange/pallas_call | solution.py:293
  29.9 1.5 %broadcast_multiply_fusion = f32[2,8,1024]{2,1,0:T(8,128)} fusion(f32[2,8,1024]{2,1,0:T(8,128)} %exchange.1), kind=kLoop, calls=%fused_computation | loop fusion | flops 16384 | bytes 131072 | tf_op jit(solution)/shard_map/mul | solution.py:329

commit v3 on v2

--- a/solution.py
+++ b/solution.py
@@ -29,8 +29,7 @@
     in_a,
     out_d,
     in_d,
-    out_t,
-    in_t,
+    total,
     tab_pair,
     tab_orb,
     idx_pair,
@@ -39,8 +38,6 @@
     recv_a,
     send_d,
     recv_d,
-    send_t,
-    recv_t,
     send_p,
     recv_p,
     send_i,
@@ -59,14 +56,17 @@
     def each_orb(body):
         lax.fori_loop(1, n_orb, lambda k, c: (body(lax.rem(me + k, n_orb)), c)[1], 0)
 
-    def each_back(body):
-        lax.fori_loop(1, n_orb, lambda k, c: (body(lax.rem(me + n_orb - k, n_orb)), c)[1], 0)
-
     def each_pair(body):
         lax.fori_loop(1, n_pair, lambda k, c: (body(lax.rem(mine + k, n_pair)), c)[1], 0)
 
-    each_orb(lambda o: pl.semaphore_signal(barrier, inc=1, device_id={"orb": o}))
-    each_pair(lambda q: pl.semaphore_signal(barrier, inc=1, device_id={"pair": q}))
+    def greet(k, c):
+        other = lax.rem(me * n_pair + mine + k, n_orb * n_pair)
+        pl.semaphore_signal(
+            barrier, inc=1, device_id={"orb": other // n_pair, "pair": lax.rem(other, n_pair)}
+        )
+        return c
+
+    lax.fori_loop(1, n_orb * n_pair, greet, 0)
 
     tab_pair[SEND, mine] = send_ref[0]
     tab_pair[LEFT, mine] = left_ref[0]
@@ -102,7 +102,7 @@
     prod[...] = jnp.zeros(prod.shape, f32)
     left_sum[...] = jnp.zeros(left_sum.shape, f32)
 
-    pl.semaphore_wait(barrier, n_orb - 1 + n_pair - 1)
+    pl.semaphore_wait(barrier, n_orb * n_pair - 1)
 
     def copy_p(q, row):
         return pltpu.make_async_remote_copy(
@@ -113,14 +113,24 @@
             device_id={"pair": q},
         )
 
-    def copy_a(o, slot):
+    fold = 2 if n_orb % 2 == 0 else 1
+    lines = n_orb // fold
+    high, low = me // fold, lax.rem(me, fold)
+
+    def copy_a(block, key, o):
         return pltpu.make_async_remote_copy(
-            src_ref=in_a.at[me],
-            dst_ref=in_a.at[slot],
-            send_sem=send_a.at[o],
-            recv_sem=recv_a.at[slot],
+            src_ref=in_a.at[block],
+            dst_ref=in_a.at[block],
+            send_sem=send_a.at[key],
+            recv_sem=recv_a.at[block],
             device_id={"orb": o},
         )
+
+    def peer(k, side):
+        return lax.rem(high + k + lines, lines) * fold + lax.rem(low + side, fold)
+
+    def along(body, start=1):
+        lax.fori_loop(start, lines, lambda k, c: (body(k), c)[1], 0)
 
     def copy_i(o, slot):
         return pltpu.make_async_remote_copy(
@@ -131,26 +141,19 @@
             device_id={"orb": o},
         )
 
-    def copy_d(o, slot):
+    def copy_d(o, q, slot, row):
         return pltpu.make_async_remote_copy(
-            src_ref=out_d.at[o],
-            dst_ref=in_d.at[slot],
-            send_sem=send_d.at[o],
-            recv_sem=recv_d.at[slot],
-            device_id={"orb": o},
-        )
-
-    def copy_t(q, slot):
-        return pltpu.make_async_remote_copy(
-            src_ref=out_t.at[q],
-            dst_ref=in_t.at[slot],
-            send_sem=send_t.at[q],
-            recv_sem=recv_t.at[slot],
-            device_id={"pair": q},
+            src_ref=out_d.at[o, q],
+            dst_ref=in_d.at[slot, row],
+            send_sem=send_d.at[o, q],
+            recv_sem=recv_d.at[slot, row],
+            device_id={"orb": o, "pair": q},
         )
 
     each_pair(lambda q: copy_p(q, mine).start())
-    each_orb(lambda o: copy_a(o, me).start())
+    if fold > 1:
+        copy_a(me, peer(0, 1), peer(0, 1)).start()
+    along(lambda k: copy_a(me, peer(k, 0), peer(k, 0)).start())
     each_pair(lambda q: copy_p(q, q).wait_recv())
     each_orb(lambda o: copy_i(o, me).start())
     tab_orb[me] = tab_pair[SEND]
@@ -236,44 +239,68 @@
     fetch_orb.start()
     fetch_orb.wait()
 
+    blocks = owned * groups
+
+    def parts(ref, s):
+        for q in range(n_pair):
+            rows = ref[:, :, q * own_rows : (q + 1) * own_rows, :]
+            out_d[s, q] = rows.reshape(blocks * own_rows, LANES).astype(bf16)
+
+    def every(body):
+        lax.fori_loop(0, n_pair, lambda q, c: (body(q), c)[1], 0)
+
     def slot(s):
-        copy_a(s, s).wait_recv()
         process(s, lambda p: idx_orb[s, p, 0, me])
-        out_d[s] = right_sum[...].astype(bf16)
-        copy_d(s, me).start()
-
-    each_back(slot)
+        parts(right_sum, s)
+        every(lambda q: copy_d(s, q, me, mine).start())
+
+    def on_line(k):
+        s = peer(-k, 0)
+        copy_a(s, s, s).wait_recv()
+        if fold > 1:
+            copy_a(s, peer(-k, 1), peer(0, 1)).start()
+        slot(s)
+
+    def across(k):
+        s = peer(-k, 1)
+        copy_a(s, s, s).wait_recv()
+        slot(s)
+
+    along(on_line)
+    if fold > 1:
+        along(across, 0)
+
+    parts(left_sum, me)
+    each_pair(lambda q: copy_d(me, q, me, mine).start())
+    for q in range(n_pair):
+        total[q] = jnp.zeros(total.shape[1:], f32)
+    total[mine] = out_d[me, mine].astype(f32)
 
     def add(s):
-        copy_d(s, s).wait_recv()
-        left_sum[...] = left_sum[...] + in_d[s].astype(f32)
-
-    each_orb(add)
-
-    blocks = owned * groups
+        def one(q):
+            copy_d(s, q, s, q).wait_recv()
+            total[q] = total[q] + in_d[s, q].astype(f32)
+
+        return one
+
+    each_orb(lambda s: every(add(s)))
+    each_pair(add(me))
     for q in range(n_pair):
-        rows = left_sum[:, :, q * own_rows : (q + 1) * own_rows, :]
-        out_t[q] = rows.reshape(blocks * own_rows, LANES).astype(bf16)
-    in_t[mine] = out_t[mine]
-    each_pair(lambda q: copy_t(q, mine).start())
-    each_pair(lambda q: copy_t(q, q).wait_recv())
-    for q in range(n_pair):
-        rows = in_t[q].astype(f32)
         for b in range(owned):
             for g in range(groups):
                 at = (b * groups + g) * own_rows
-                out_ref[b, :, (q * groups + g) * LANES : (q * groups + g + 1) * LANES] = rows[
-                    at : at + own_rows
+                out_ref[b, :, (q * groups + g) * LANES : (q * groups + g + 1) * LANES] = total[
+                    q, at : at + own_rows, :
                 ]
 
     def drain_orb(o):
-        copy_a(o, me).wait_send()
+        copy_a(me, o, o).wait_send()
         copy_i(o, me).wait_send()
-        copy_d(o, me).wait_send()
+        every(lambda q: copy_d(o, q, me, mine).wait_send())
 
     def drain_pair(q):
         copy_p(q, mine).wait_send()
-        copy_t(q, mine).wait_send()
+        copy_d(me, q, me, mine).wait_send()
 
     each_orb(drain_orb)
     each_pair(drain_pair)
@@ -303,20 +330,17 @@
             pltpu.VMEM(dense, f32),
             pltpu.VMEM(dense, f32),
             pltpu.VMEM((n_orb, owned * groups + 1, box_side, LANES), bf16),
-            pltpu.VMEM((n_orb, *dense), bf16),
-            pltpu.VMEM((n_orb, *dense), bf16),
-            pltpu.VMEM((n_pair, owned * groups * own_rows, LANES), bf16),
-            pltpu.VMEM((n_pair, owned * groups * own_rows, LANES), bf16),
+            pltpu.VMEM((n_orb, n_pair, owned * groups * own_rows, LANES), bf16),
+            pltpu.VMEM((n_orb, n_pair, owned * groups * own_rows, LANES), bf16),
+            pltpu.VMEM((n_pair, owned * groups * own_rows, LANES), f32),
             pltpu.VMEM((3, n_pair, 1, slots), i32),
             pltpu.VMEM((n_orb, n_pair, 1, slots), i32),
             pltpu.SMEM((3, n_pair, 1, slots), i32),
             pltpu.SMEM((n_orb, n_pair, 1, slots), i32),
             dma((n_orb,)),
             dma((n_orb,)),
-            dma((n_orb,)),
-            dma((n_orb,)),
-            dma((n_pair,)),
-            dma((n_pair,)),
+            dma((n_orb, n_pair)),
+            dma((n_orb, n_pair)),
             dma((n_pair,)),
             dma((n_pair,)),
             dma((n_orb,)),

time: 31.5 us -> 28 us (0.89)
  Pallas kernels: 29.9 us -> 26.3 us
    pallas_call x1, Pallas kernels: 29.9 us -> 26.3 us  [local(): pl.pallas_call(functools.partial(kernel, n_orb, n_pair), out_shape=jax.Sh...]
where the time goes in v3:
time: 28 us; the launch traced here: 27.8 us
  Pallas kernels  26.3 us (94%)
  other arithmetic  1.47 us (5%)
    pallas_call x1, Pallas kernels, local(): pl.pallas_call(functools.partial(kernel, n_orb, n_pair), out_shape=jax.Sh...  26.3 us
    mul x1, other arithmetic, local(): return -0.25 * field  1.47 us

profile of v3, /device:TPU:0, one launch (start us, length us, event | category | flops | bytes accessed | tf_op | source)
XLA Modules:
  0.0 27.8 jit_solution(3982444874456218418)
XLA Ops:
  0.0 26.3 %exchange.1 = f32[2,8,1024]{2,1,0:T(8,128)} custom-call(f32[2,32,1024]{2,1,0:T(8,128)} %orb_ref.1, s32[1,1,8]{2,1,0:T(1,128)} %send_ref.1, s32[1,1,8]{2,1,0:T(1,128)} %left_ref.1, s32[1,1,8]{2,1,0:T(1,128)} %off_ref.1), custom_call_target="tpu_custom_call" | custom-call | tf_op jit(solution)/shard_map/exchange/pallas_call | solution.py:320
  26.4 1.5 %broadcast_multiply_fusion = f32[2,8,1024]{2,1,0:T(8,128)} fusion(f32[2,8,1024]{2,1,0:T(8,128)} %exchange.1), kind=kLoop, calls=%fused_computation | loop fusion | flops 16384 | bytes 131072 | tf_op jit(solution)/shard_map/mul | solution.py:353

commit v4 on v3

--- a/solution.py
+++ b/solution.py
@@ -9,7 +9,7 @@
 
 LANES = 128
 SUBS = 8
-SEND, LEFT, OFFSET = 0, 1, 2
+LEFT, OFFSET = 0, 1
 
 
 def kernel(
@@ -68,7 +68,7 @@
 
     lax.fori_loop(1, n_orb * n_pair, greet, 0)
 
-    tab_pair[SEND, mine] = send_ref[0]
+    tab_orb[me, mine] = send_ref[0]
     tab_pair[LEFT, mine] = left_ref[0]
     tab_pair[OFFSET, mine] = off_ref[0]
 
@@ -132,14 +132,17 @@
     def along(body, start=1):
         lax.fori_loop(start, lines, lambda k, c: (body(k), c)[1], 0)
 
-    def copy_i(o, slot):
+    def copy_i(o, q, slot, row):
         return pltpu.make_async_remote_copy(
-            src_ref=tab_pair.at[SEND],
-            dst_ref=tab_orb.at[slot],
-            send_sem=send_i.at[o],
-            recv_sem=recv_i.at[slot],
-            device_id={"orb": o},
-        )
+            src_ref=tab_orb.at[me, mine],
+            dst_ref=tab_orb.at[slot, row],
+            send_sem=send_i.at[o, q],
+            recv_sem=recv_i.at[slot, row],
+            device_id={"orb": o, "pair": q},
+        )
+
+    def every(body):
+        lax.fori_loop(0, n_pair, lambda q, c: (body(q), c)[1], 0)
 
     def copy_d(o, q, slot, row):
         return pltpu.make_async_remote_copy(
@@ -151,15 +154,19 @@
         )
 
     each_pair(lambda q: copy_p(q, mine).start())
+    each_pair(lambda q: copy_i(me, q, me, mine).start())
+    each_orb(lambda o: every(lambda q: copy_i(o, q, me, mine).start()))
     if fold > 1:
         copy_a(me, peer(0, 1), peer(0, 1)).start()
     along(lambda k: copy_a(me, peer(k, 0), peer(k, 0)).start())
     each_pair(lambda q: copy_p(q, q).wait_recv())
-    each_orb(lambda o: copy_i(o, me).start())
-    tab_orb[me] = tab_pair[SEND]
-    fetch = pltpu.make_async_copy(tab_pair, idx_pair, local_sem)
+    each_pair(lambda q: copy_i(me, q, me, q).wait_recv())
+    fetch = pltpu.make_async_copy(tab_pair, idx_pair, local_sem.at[0])
+    fetch_own = pltpu.make_async_copy(tab_orb.at[me], idx_orb.at[me], local_sem.at[1])
     fetch.start()
+    fetch_own.start()
     fetch.wait()
+    fetch_own.wait()
 
     tile = (SUBS, LANES)
     lane = lax.broadcasted_iota(jnp.int32, tile, 1)
@@ -231,11 +238,11 @@
 
         lax.fori_loop(0, n_pair, route, 0)
 
-    process(me, lambda p: idx_pair[SEND, p, 0, me])
+    process(me, lambda p: idx_orb[me, p, 0, me])
     left_sum[...] = left_sum[...] + right_sum[...]
 
-    each_orb(lambda o: copy_i(o, o).wait_recv())
-    fetch_orb = pltpu.make_async_copy(tab_orb, idx_orb, local_sem)
+    each_orb(lambda o: every(lambda q: copy_i(o, q, o, q).wait_recv()))
+    fetch_orb = pltpu.make_async_copy(tab_orb, idx_orb, local_sem.at[0])
     fetch_orb.start()
     fetch_orb.wait()
 
@@ -245,9 +252,6 @@
         for q in range(n_pair):
             rows = ref[:, :, q * own_rows : (q + 1) * own_rows, :]
             out_d[s, q] = rows.reshape(blocks * own_rows, LANES).astype(bf16)
-
-    def every(body):
-        lax.fori_loop(0, n_pair, lambda q, c: (body(q), c)[1], 0)
 
     def slot(s):
         process(s, lambda p: idx_orb[s, p, 0, me])
@@ -295,11 +299,12 @@
 
     def drain_orb(o):
         copy_a(me, o, o).wait_send()
-        copy_i(o, me).wait_send()
+        every(lambda q: copy_i(o, q, me, mine).wait_send())
         every(lambda q: copy_d(o, q, me, mine).wait_send())
 
     def drain_pair(q):
         copy_p(q, mine).wait_send()
+        copy_i(me, q, me, mine).wait_send()
         copy_d(me, q, me, mine).wait_send()
 
     each_orb(drain_orb)
@@ -333,9 +338,9 @@
             pltpu.VMEM((n_orb, n_pair, owned * groups * own_rows, LANES), bf16),
             pltpu.VMEM((n_orb, n_pair, owned * groups * own_rows, LANES), bf16),
             pltpu.VMEM((n_pair, owned * groups * own_rows, LANES), f32),
-            pltpu.VMEM((3, n_pair, 1, slots), i32),
+            pltpu.VMEM((2, n_pair, 1, slots), i32),
             pltpu.VMEM((n_orb, n_pair, 1, slots), i32),
-            pltpu.SMEM((3, n_pair, 1, slots), i32),
+            pltpu.SMEM((2, n_pair, 1, slots), i32),
             pltpu.SMEM((n_orb, n_pair, 1, slots), i32),
             dma((n_orb,)),
             dma((n_orb,)),
@@ -343,9 +348,9 @@
             dma((n_orb, n_pair)),
             dma((n_pair,)),
             dma((n_pair,)),
-            dma((n_orb,)),
-            dma((n_orb,)),
-            dma(()),
+            dma((n_orb, n_pair)),
+            dma((n_orb, n_pair)),
+            dma((2,)),
         ],
         compiler_params=pltpu.CompilerParams(collective_id=0, has_side_effects=True),
         name="exchange",

time: 28 us -> 27 us (0.964)
  Pallas kernels: 26.3 us -> 25.4 us
    pallas_call x1, Pallas kernels: 26.3 us -> 25.4 us  [local(): pl.pallas_call(functools.partial(kernel, n_orb, n_pair), out_shape=jax.Sh...]
where the time goes in v4:
time: 27 us; the launch traced here: 26.9 us
  Pallas kernels  25.4 us (94%)
  other arithmetic  1.47 us (5%)
    pallas_call x1, Pallas kernels, local(): pl.pallas_call(functools.partial(kernel, n_orb, n_pair), out_shape=jax.Sh...  25.4 us
    mul x1, other arithmetic, local(): return -0.25 * field  1.47 us

profile of v4, /device:TPU:0, one launch (start us, length us, event | category | flops | bytes accessed | tf_op | source)
XLA Modules:
  0.0 26.9 jit_solution(18406818699261678252)
XLA Ops:
  0.0 25.4 %exchange.1 = f32[2,8,1024]{2,1,0:T(8,128)} custom-call(f32[2,32,1024]{2,1,0:T(8,128)} %orb_ref.1, s32[1,1,8]{2,1,0:T(1,128)} %send_ref.1, s32[1,1,8]{2,1,0:T(1,128)} %left_ref.1, s32[1,1,8]{2,1,0:T(1,128)} %off_ref.1), custom_call_target="tpu_custom_call" | custom-call | tf_op jit(solution)/shard_map/exchange/pallas_call | solution.py:325
  25.4 1.5 %broadcast_multiply_fusion = f32[2,8,1024]{2,1,0:T(8,128)} fusion(f32[2,8,1024]{2,1,0:T(8,128)} %exchange.1), kind=kLoop, calls=%fused_computation | loop fusion | flops 16384 | bytes 131072 | tf_op jit(solution)/shard_map/mul | solution.py:358

commit v5 on v4

--- a/solution.py
+++ b/solution.py
@@ -159,6 +159,14 @@
     if fold > 1:
         copy_a(me, peer(0, 1), peer(0, 1)).start()
     along(lambda k: copy_a(me, peer(k, 0), peer(k, 0)).start())
+    def hand_over(k):
+        s = peer(-k, 0)
+        copy_a(s, s, s).wait_recv()
+        if fold > 1:
+            copy_a(s, peer(-k, 1), peer(0, 1)).start()
+
+    if lines > 1:
+        hand_over(1)
     each_pair(lambda q: copy_p(q, q).wait_recv())
     each_pair(lambda q: copy_i(me, q, me, q).wait_recv())
     fetch = pltpu.make_async_copy(tab_pair, idx_pair, local_sem.at[0])
@@ -259,11 +267,11 @@
         every(lambda q: copy_d(s, q, me, mine).start())
 
     def on_line(k):
-        s = peer(-k, 0)
-        copy_a(s, s, s).wait_recv()
-        if fold > 1:
-            copy_a(s, peer(-k, 1), peer(0, 1)).start()
-        slot(s)
+        @pl.when(k + 1 < lines)
+        def _():
+            hand_over(k + 1)
+
+        slot(peer(-k, 0))
 
     def across(k):
         s = peer(-k, 1)

time: 27 us -> 26.5 us (0.981)
  Pallas kernels: 25.4 us -> 24.8 us
    pallas_call x1, Pallas kernels: 25.4 us -> 24.8 us  [local(): pl.pallas_call(functools.partial(kernel, n_orb, n_pair), out_shape=jax.Sh...]
where the time goes in v5:
time: 26.5 us; the launch traced here: 26.3 us
  Pallas kernels  24.8 us (94%)
  other arithmetic  1.47 us (6%)
    pallas_call x1, Pallas kernels, local(): pl.pallas_call(functools.partial(kernel, n_orb, n_pair), out_shape=jax.Sh...  24.8 us
    mul x1, other arithmetic, local(): return -0.25 * field  1.47 us

profile of v5, /device:TPU:0, one launch (start us, length us, event | category | flops | bytes accessed | tf_op | source)
XLA Modules:
  0.0 26.3 jit_solution(7005588165346787238)
XLA Ops:
  0.0 24.8 %exchange.1 = f32[2,8,1024]{2,1,0:T(8,128)} custom-call(f32[2,32,1024]{2,1,0:T(8,128)} %orb_ref.1, s32[1,1,8]{2,1,0:T(1,128)} %send_ref.1, s32[1,1,8]{2,1,0:T(1,128)} %left_ref.1, s32[1,1,8]{2,1,0:T(1,128)} %off_ref.1), custom_call_target="tpu_custom_call" | custom-call | tf_op jit(solution)/shard_map/exchange/pallas_call | solution.py:333
  24.9 1.5 %broadcast_multiply_fusion = f32[2,8,1024]{2,1,0:T(8,128)} fusion(f32[2,8,1024]{2,1,0:T(8,128)} %exchange.1), kind=kLoop, calls=%fused_computation | loop fusion | flops 16384 | bytes 131072 | tf_op jit(solution)/shard_map/mul | solution.py:366
